TPU v7x, 512 devices: a whole 4x4x16 slice. The times are simulated.
512 devices in a mesh: sx: 32 (over z_hi, y, core), sy: 16 (over x, z_lo).
Axes of the slice: x: 4, y: 4, z: 16 (z_hi: 4, z_lo: 4; z = z_hi * 4 + z_lo), core: 2. Of those that a mesh axis runs over, the one named last changes fastest.
Arguments:
- forward_prop: bfloat16 [2, 2, 12, 12, 64, 4096], P(None, None, None, None, 'sx', 'sy'), may hold values from -0.08984375 to 0.08984375
- backward_prop: bfloat16 [2, 2, 12, 12, 64, 4096], P(None, None, None, None, 'sx', 'sy'), may hold values from -0.08984375 to 0.08984375
- gamma_table: int32 [16, 4, 2], replicated, may hold values from 0 to 3, as said below
- source_site: int32 [3], replicated, may hold values from 0 to 63
- momenta: int32 [32, 3], replicated, may hold values from -8 to 7
Outputs:
- corr: float32 [16, 2, 2, 64, 4096], P(None, None, None, 'sx', 'sy')
- listed: float32 [2, 16, 2, 32], replicated
Inputs may be any that keep to these rules, and one draw needn't show every extreme that they name: For every insertion g, gamma_table[g, 0..3, 0] is a permutation of 0..3; gamma_table[g, s, 1] is the power of i of that entry.
All inputs are finite; a program needn't handle non-finite values.
Results may differ from a plain program's by a relative error of at most 0.0003.
Values sent between devices are 32-bit elements; how exact they have to be, the bound alone decides.
A program may use at most 64 MiB of HBM per device.

v0:
```python
import math
import jax
import jax.numpy as jnp
from jax import lax
from jax.sharding import PartitionSpec as P

L = 64
LZ = 64
HIGHEST = lax.Precision.HIGHEST


def gamma_matrices(gamma_table):
    inserts = gamma_table.shape[0]
    columns = gamma_table[:, :, 0]
    powers = gamma_table[:, :, 1]
    spin_ids = jnp.arange(4, dtype=jnp.int32)
    matches = (columns[:, :, None] == spin_ids[None, None, :]).astype(jnp.float32)
    unit_re = (powers == 0).astype(jnp.float32) - (powers == 2).astype(jnp.float32)
    unit_im = (powers == 1).astype(jnp.float32) - (powers == 3).astype(jnp.float32)
    return (
        (matches * unit_re[:, :, None]).reshape(inserts, 16),
        (matches * unit_im[:, :, None]).reshape(inserts, 16),
    )


def dft_table(length, anchor):
    wavenum = jnp.arange(length, dtype=jnp.int32)
    offsets = jnp.mod(wavenum - anchor, length)
    phase_index = jnp.mod(offsets[:, None] * wavenum[None, :], length)
    angles = 2.0 * math.pi / length * phase_index.astype(jnp.float32)
    return (jnp.cos(angles), -jnp.sin(angles))


def complex_step(real_part, imag_part, table_re, table_im, pattern):
    out_re = jnp.einsum(pattern, real_part, table_re, precision=HIGHEST) - jnp.einsum(
        pattern, imag_part, table_im, precision=HIGHEST
    )
    out_im = jnp.einsum(pattern, real_part, table_im, precision=HIGHEST) + jnp.einsum(
        pattern, imag_part, table_re, precision=HIGHEST
    )
    return (out_re, out_im)


def transform(fields, source_site):
    table_re, table_im = dft_table(fields.shape[4], source_site[2])
    along_z = jnp.stack(
        complex_step(fields[:, 0], fields[:, 1], table_re, table_im, "nabz,zk->nabk"), 1
    )
    depth_share = along_z.shape[4] // lax.axis_size("sy")
    first_depth = lax.axis_index("sy") * depth_share
    length_y = along_z.shape[3] * lax.axis_size("sy")
    full_re, full_im = dft_table(length_y, source_site[1])
    part = lax.dynamic_slice_in_dim(
        lax.all_gather(along_z, "sy", axis=3, tiled=True), first_depth, depth_share, 4
    )
    step_re, step_im = complex_step(part[:, 0], part[:, 1], full_re, full_im, "nayc,yk->nakc")
    along_y = jnp.stack([step_re, step_im], 1)
    arrived = lax.all_to_all(along_y, "sx", split_axis=3, concat_axis=2, tiled=True)
    table_re, table_im = dft_table(arrived.shape[2], source_site[0])
    along_x = complex_step(arrived[:, 0], arrived[:, 1], table_re, table_im, "nxbc,xk->nbck")
    return jnp.stack(along_x, 1)


def apply_gammas(mat_re, mat_im, real_part, imag_part):
    extent = real_part.shape
    flat_re = real_part.reshape(extent[0], -1)
    flat_im = imag_part.reshape(extent[0], -1)
    out_re = jnp.dot(mat_re, flat_re, precision=HIGHEST) - jnp.dot(
        mat_im, flat_im, precision=HIGHEST
    )
    out_im = jnp.dot(mat_re, flat_im, precision=HIGHEST) + jnp.dot(
        mat_im, flat_re, precision=HIGHEST
    )
    return (out_re.reshape(extent), out_im.reshape(extent))


def project_sites(fields, source_site, momenta, rows_x, rows_y, length, depth):
    coord_x = lax.axis_index("sx") * rows_x + jnp.arange(rows_x, dtype=jnp.int32) - source_site[0]
    coord_y = lax.axis_index("sy") * rows_y + jnp.arange(rows_y, dtype=jnp.int32) - source_site[1]
    coord_z = jnp.arange(depth, dtype=jnp.int32) - source_site[2]
    part_x = jnp.mod(momenta[:, 0:1] * coord_x[None, :], length)
    part_y = jnp.mod(momenta[:, 1:2] * coord_y[None, :], length)
    part_z = jnp.mod(momenta[:, 2:3] * coord_z[None, :], depth)
    plane = jnp.mod(part_x[:, :, None] + part_y[:, None, :], length).astype(jnp.float32)
    angles = (
        2.0 * math.pi / length * plane[:, :, :, None]
        + 2.0 * math.pi / depth * part_z.astype(jnp.float32)[:, None, None, :]
    )
    angles = angles.reshape(momenta.shape[0], -1)
    cosine = jnp.cos(angles)
    sine = jnp.sin(angles)
    field_re = fields[:, 0].reshape(fields.shape[0], -1)
    field_im = fields[:, 1].reshape(fields.shape[0], -1)
    local_re = jnp.dot(field_re, cosine.T, precision=HIGHEST) + jnp.dot(
        field_im, sine.T, precision=HIGHEST
    )
    local_im = jnp.dot(field_im, cosine.T, precision=HIGHEST) - jnp.dot(
        field_re, sine.T, precision=HIGHEST
    )
    return (local_re, local_im)


def body(forward_prop, backward_prop, gamma_table, source_site, momenta):
    slices = forward_prop.shape[0]
    rows_x = forward_prop.shape[4]
    rows_y = backward_prop.shape[5] // LZ
    inserts = gamma_table.shape[0]
    forward = forward_prop.reshape(slices, 2, 4, 3, 12, -1)
    backward = backward_prop.reshape(slices, 2, 4, 3, 12, -1)
    pattern = "tscjn,tucjn->sutn"
    pair_re = jnp.einsum(
        pattern, backward[:, 0], forward[:, 0], preferred_element_type=jnp.float32
    ) + jnp.einsum(pattern, backward[:, 1], forward[:, 1], preferred_element_type=jnp.float32)
    pair_im = jnp.einsum(
        pattern, backward[:, 0], forward[:, 1], preferred_element_type=jnp.float32
    ) - jnp.einsum(pattern, backward[:, 1], forward[:, 0], preferred_element_type=jnp.float32)
    pair_re = pair_re.reshape(16, slices, -1)
    pair_im = pair_im.reshape(16, slices, -1)
    mat_re, mat_im = gamma_matrices(gamma_table)
    field_re, field_im = apply_gammas(mat_re, mat_im, pair_re, pair_im)
    fields = jnp.stack([field_re, field_im], 2).reshape(inserts * slices, 2, rows_x, rows_y, LZ)
    spectrum = transform(fields, source_site)
    local_re, local_im = project_sites(fields, source_site, momenta, rows_x, rows_y, L, LZ)
    listed_re, listed_im = lax.psum((local_re, local_im), ("sx", "sy"))
    listed_re = listed_re.reshape(inserts, slices, -1)
    listed_im = listed_im.reshape(inserts, slices, -1)
    corr_re = spectrum[:, 0].reshape(inserts, slices, spectrum.shape[2], -1)
    corr_im = spectrum[:, 1].reshape(inserts, slices, spectrum.shape[2], -1)
    return (jnp.stack([corr_re, corr_im], 2), jnp.stack([listed_re, listed_im], 0))


def solution(mesh):
    placed = (
        P(None, None, None, None, "sx", "sy"),
        P(None, None, None, None, "sx", "sy"),
        P(),
        P(),
        P(),
    )
    return jax.shard_map(
        body,
        mesh=mesh,
        in_specs=placed,
        out_specs=(P(None, None, None, "sx", "sy"), P()),
        check_vma=False,
    )
```

profile of v0, /device:TPU:1, one launch (start us, length us, event | category | flops | bytes accessed | tf_op | source)
XLA Modules:
  0.0 323.4 jit_solution(12954592644119887692)
XLA Ops:
  7.2 0.7 fusion.92
  7.9 2.1 reshape.371
  10.0 0.8 fusion.144
  10.9 4.5 %copy.82 = bf16[2,1,4,3,12,512]{4,2,3,5,0,1:T(4,128)(2,1)S(1)} copy(bf16[2,1,4,3,12,512]{5,4,3,2,1,0:T(8,128)(2,1)} %get-tuple-element.11) | data formatting | bytes 589824
  15.3 2.8 reshape.372
  18.1 2.1 fusion.145
  20.2 5.3 %copy.83 = bf16[2,1,4,3,12,512]{4,2,3,5,0,1:T(4,128)(2,1)} copy(bf16[2,1,4,3,12,512]{5,4,3,2,1,0:T(8,128)(2,1)} %get-tuple-element.13) | data formatting | bytes 589824
  25.4 3.8 %copy.80 = bf16[2,1,4,3,12,512]{4,2,3,5,0,1:T(4,128)(2,1)} copy(bf16[2,1,4,3,12,512]{5,4,3,2,1,0:T(8,128)(2,1)S(1)} %get-tuple-element.10) | data formatting | bytes 589824
  29.2 5.3 %copy.81 = bf16[2,1,4,3,12,512]{4,2,3,5,0,1:T(4,128)(2,1)} copy(bf16[2,1,4,3,12,512]{5,4,3,2,1,0:T(8,128)(2,1)} %get-tuple-element.12) | data formatting | bytes 589824
  34.5 5.6 %fusion.2 = f32[2,512,4,4,1]{3,2,4,1,0:T(4,128)S(1)} fusion(bf16[2,1,4,3,12,512]{4,2,3,5,0,1:T(4,128)(2,1)} %copy.83, bf16[2,1,4,3,12,512]{4,2,3,5,0,1:T(4,128)(2,1)S(1)} %copy.82), kind=kOutput, calls=%fused_computation.2 | convolution fusion | flops 1179648 | bytes 655360 | tf_op jit(solution)/shard_map/tscjn,tucjn->sutn/dot_general | solution.py:113
  40.2 5.0 %fusion = f32[2,512,4,4,1]{3,2,4,1,0:T(4,128)} fusion(bf16[2,1,4,3,12,512]{4,2,3,5,0,1:T(4,128)(2,1)S(1)} %copy-done.1, bf16[2,1,4,3,12,512]{4,2,3,5,0,1:T(4,128)(2,1)S(1)} %copy-done.2), kind=kOutput, calls=%fused_computation | convolution fusion | flops 1179648 | bytes 655360 | tf_op jit(solution)/shard_map/tscjn,tucjn->sutn/dot_general | solution.py:116
  45.2 3.7 %fusion.13 = f32[4,4,2,512]{0,1,3,2:T(4,128)} fusion(f32[2,512,4,4,1]{3,2,4,1,0:T(4,128)S(1)} %fusion.2, bf16[2,1,4,3,12,512]{4,2,3,5,0,1:T(4,128)(2,1)S(1)} %copy-done, bf16[2,1,4,3,12,512]{4,2,3,5,0,1:T(4,128)(2,1)S(1)} %copy-done.2), kind=kOutput, calls=%fused_computation.17 | convolution fusion | flops 1196032 | bytes 720896 | tf_op jit(solution)/shard_map/tscjn,tucjn->sutn/dot_general | solution.py:111
  48.8 2.1 copy.48
  51.0 7.5 %fusion.12 = f32[4,4,2,512]{0,1,3,2:T(4,128)} fusion(f32[2,512,4,4,1]{3,2,4,1,0:T(4,128)} %fusion, bf16[2,1,4,3,12,512]{4,2,3,5,0,1:T(4,128)(2,1)} %copy.81, bf16[2,1,4,3,12,512]{4,2,3,5,0,1:T(4,128)(2,1)S(1)} %copy.82), kind=kOutput, calls=%fused_computation.15 | convolution fusion | flops 1196032 | bytes 720896 | tf_op jit(solution)/shard_map/tscjn,tucjn->sutn/dot_general | solution.py:114
  58.5 1.9 copy.49
  60.5 0.7 fusion.146
  62.0 1.3 and_select_fusion.1
  65.5 0.7 pad_maximum_fusion
  66.3 0.6 iota_subtract_fusion
  67.0 0.7 add_subtract_fusion.1
  67.6 0.7 add_subtract_fusion
  68.7 1.1 add_sine_fusion
  70.0 0.7 and_select_fusion.3
  71.1 107.5 %all-gather.2.cloned.1.call-done = f32[32,2,2,64,64]{4,0,3,2,1:T(8,128)} async-done(((f32[32,2,2,4,64]{4,0,3,2,1:T(8,128)}), f32[32,2,2,64,64]{4,0,3,2,1:T(8,128)}) %all-gather.2.cloned.1.call-update) | async-done | bytes 2097168 | tf_op jit(solution)/shard_map/all_gather | solution.py:54
  178.6 4.7 %dynamic-slice_bitcast_fusion = (f32[32,2,64,4]{3,0,2,1:T(8,128)S(1)}, f32[32,2,64,4]{3,0,2,1:T(8,128)}) fusion(f32[32,2,2,64,64]{4,0,3,2,1:T(8,128)} %all-gather.2.cloned.1.call-done, s32[]{:T(128)S(6)} %add.213, s32[]{:T(128)S(6)} %select_n.88), kind=kLoop, calls=%fused_computation.12 | loop fusion | bytes 262152 | tf_op jit(solution)/shard_map/squeeze | solution.py:56
  183.3 2.6 copy.54
  186.9 1.2 copy.55
  189.4 1.0 reshape.373
  190.4 13.0 %all-to-all-start = ((f32[32,1,1024]{2,1,0:T(1,128)}), f32[32,1,1024]{2,1,0:T(1,128)S(1)}, u32[]{:S(2)}, u32[]{:S(2)}) async-start(f32[32,1,1024]{2,1,0:T(1,128)} %reshape.373), calls=%async_computation | async-start | bytes 262144 | tf_op jit(solution)/shard_map/all_to_all | solution.py:58
  203.8 106.2 %all-reduce = (f32[1,16,2,32]{3,2,1,0:T(2,128)S(1)}, f32[1,16,2,32]{3,2,1,0:T(2,128)S(1)}) all-reduce(f32[1,16,2,32]{3,2,1,0:T(2,128)S(1)} %bitcast.184, f32[1,16,2,32]{3,2,1,0:T(2,128)S(1)} %bitcast.183), channel_id=1, replica_groups=mesh['sx'=32,'sy'=16] {'sx','sy'}, use_global_device_ids=true, to_apply=%region_1.2 | all-reduce | flops 2048 | bytes 16384 | tf_op jit(solution)/shard_map/psum | solution.py:124
  311.1 0.9 reduce
  315.9 0.7 copy.65
  (61 shorter events, 11.7 us)
Async XLA Ops:
  7.2 171.4 %all-gather.2.cloned.1.call-start = ((), (), s32[]{:S(2)}) async-start(), calls=%async_computation.1 | async-start | bytes 4456448 | tf_op jit(solution)/shard_map/all_gather | solution.py:54
  34.5 5.6 %copy-start.1 = (bf16[2,1,4,3,12,512]{4,2,3,5,0,1:T(4,128)(2,1)S(1)}, bf16[2,1,4,3,12,512]{4,2,3,5,0,1:T(4,128)(2,1)}, u32[]{:S(2)}) copy-start(bf16[2,1,4,3,12,512]{4,2,3,5,0,1:T(4,128)(2,1)} %copy.83) | copy-start | bytes 884740
  34.5 5.6 %copy-start.2 = (bf16[2,1,4,3,12,512]{4,2,3,5,0,1:T(4,128)(2,1)S(1)}, bf16[2,1,4,3,12,512]{4,2,3,5,0,1:T(4,128)(2,1)}, u32[]{:S(2)}) copy-start(bf16[2,1,4,3,12,512]{4,2,3,5,0,1:T(4,128)(2,1)} %copy.80) | copy-start | bytes 884740
  40.2 5.0 %copy-start = (bf16[2,1,4,3,12,512]{4,2,3,5,0,1:T(4,128)(2,1)S(1)}, bf16[2,1,4,3,12,512]{4,2,3,5,0,1:T(4,128)(2,1)}, u32[]{:S(2)}) copy-start(bf16[2,1,4,3,12,512]{4,2,3,5,0,1:T(4,128)(2,1)} %copy.81) | copy-start | bytes 884740
  50.9 9.5 %copy-start.3 = (s32[3]{0:T(128)S(1)}, s32[3]{0:T(128)}, u32[]{:S(2)}) copy-start(s32[3]{0:T(128)} %param.8) | copy-start | bytes 40
  50.9 10.2 %slice-start = ((s32[16,4,2]{0,2,1:T(2,128)}), s32[16,4,1]{0,2,1:T(1,128)S(1)}, s32[]{:S(2)}) async-start(s32[16,4,2]{0,2,1:T(2,128)} %param.7), calls=%async_computation.2 | async-start | bytes 4096 | tf_op jit(solution)/shard_map/slice | solution.py:14
  58.5 9.8 %copy-start.4 = (s32[32,3]{0,1:T(4,128)S(1)}, s32[32,3]{0,1:T(4,128)}, u32[]{:S(2)}) copy-start(s32[32,3]{0,1:T(4,128)} %param.9) | copy-start | bytes 1156
  190.4 120.2 %all-to-all-start = ((f32[32,1,1024]{2,1,0:T(1,128)}), f32[32,1,1024]{2,1,0:T(1,128)S(1)}, u32[]{:S(2)}, u32[]{:S(2)}) async-start(f32[32,1,1024]{2,1,0:T(1,128)} %reshape.373), calls=%async_computation | async-start | bytes 262144 | tf_op jit(solution)/shard_map/all_to_all | solution.py:58
Sparse Core Ops, SparseCore 0:
  66.4 112.1 all-gather.1
where the time goes:
time: 325 us; the launch traced here: 323 us
  waiting for transfers between devices  108 us (33%)
  blocking collectives  106 us (33%)
  local copies, waits for them, and re-layouts  44.1 us (14%)
  matrix products  29.7 us (9%)
  between operations  14.4 us (4%)
  starting transfers between devices  13 us (4%)
  other arithmetic  8.45 us (3%)
    all_gather x1, waiting for transfers between devices, transform(): lax.all_gather(along_z, 'sy', axis=3, tiled=True)  107 us
    psum x1, blocking collectives, body(): listed_re, listed_im = lax.psum((local_re, local_im), ('sx', 'sy'))  106 us
    unnamed x19, local copies, waits for them, and re-layouts  20.8 us
    all_to_all x1, starting transfers between devices, transform(): lax.all_to_all(along_y, 'sx', split_axis=3, concat_axis=2, tiled=True)  13 us
    dot_general x1, matrix products, body(): jnp.einsum(pattern, backward[:, 0], forward[:, 1], preferred_element_type...  7.53 us
  transfers between devices with their start and end apart: 2, of which 1 were waited for; matrix products, arithmetic and copies ran while one was open for 2% of the time, Pallas kernels for 0%

commit v1 on v0

--- a/solution.py
+++ b/solution.py
@@ -3,10 +3,17 @@
 import jax.numpy as jnp
 from jax import lax
 from jax.sharding import PartitionSpec as P
+from jax.lax import all_to_all, axis_size
 
 L = 64
 LZ = 64
 HIGHEST = lax.Precision.HIGHEST
+
+
+def switch_the_masks(base_x, ax_name):
+    z = jnp.stack(axis_size(ax_name) * [base_x])
+    step_out = all_to_all(z, ax_name, 0, 0)
+    return jnp.concatenate(step_out, axis=3)
 
 
 def gamma_matrices(gamma_table):
@@ -50,9 +57,7 @@
     first_depth = lax.axis_index("sy") * depth_share
     length_y = along_z.shape[3] * lax.axis_size("sy")
     full_re, full_im = dft_table(length_y, source_site[1])
-    part = lax.dynamic_slice_in_dim(
-        lax.all_gather(along_z, "sy", axis=3, tiled=True), first_depth, depth_share, 4
-    )
+    part = lax.dynamic_slice_in_dim(switch_the_masks(along_z, "sy"), first_depth, depth_share, 4)
     step_re, step_im = complex_step(part[:, 0], part[:, 1], full_re, full_im, "nayc,yk->nakc")
     along_y = jnp.stack([step_re, step_im], 1)
     arrived = lax.all_to_all(along_y, "sx", split_axis=3, concat_axis=2, tiled=True)

time: 325 us -> 279 us (0.86)
  waiting for transfers between devices: 108 us -> 44.9 us
  between operations: 14.4 us -> 1.08 us
  starting transfers between devices: 13 us -> 25.8 us
  local copies, waits for them, and re-layouts: 44.1 us -> 56.9 us
  other arithmetic: 8.45 us -> 15.2 us
    all_gather x1 -> x0, waiting for transfers between devices: 107 us -> none  [transform(): lax.all_gather(along_z, 'sy', axis=3, tiled=True)]
    all_to_all x0 -> x1, waiting for transfers between devices: none -> 44.9 us  [switch_the_masks(): step_out = all_to_all(z, ax_name, 0, 0)]
    unnamed x19 -> x26, local copies, waits for them, and re-layouts: 20.8 us -> 36.9 us
    all_to_all x0 -> x1, starting transfers between devices: none -> 9.14 us  [switch_the_masks(): step_out = all_to_all(z, ax_name, 0, 0)]
    squeeze x3 -> x0, local copies, waits for them, and re-layouts: 8.52 us -> none  [the longest x2 5.88 us: transform(): part[:, 1]]
    all_to_all x0 -> x1, other arithmetic: none -> 7.32 us  [switch_the_masks(): step_out = all_to_all(z, ax_name, 0, 0)]
    all_to_all x1, starting transfers between devices: 13 us -> 16.7 us  [transform(): lax.all_to_all(along_y, 'sx', split_axis=3, concat_axis=2, tiled=True)]
    all_to_all x0 -> x2, local copies, waits for them, and re-layouts: none -> 3.26 us  [switch_the_masks(): step_out = all_to_all(z, ax_name, 0, 0)]
where the time goes in v1:
time: 279 us; the launch traced here: 278 us
  blocking collectives  104 us (37%)
  local copies, waits for them, and re-layouts  56.9 us (20%)
  waiting for transfers between devices  44.9 us (16%)
  matrix products  29.7 us (11%)
  starting transfers between devices  25.8 us (9%)
  other arithmetic  15.2 us (5%)
    psum x1, blocking collectives, body(): listed_re, listed_im = lax.psum((local_re, local_im), ('sx', 'sy'))  104 us
    all_to_all x1, waiting for transfers between devices, switch_the_masks(): step_out = all_to_all(z, ax_name, 0, 0)  44.9 us
    unnamed x26, local copies, waits for them, and re-layouts  36.9 us
    all_to_all x1, starting transfers between devices, transform(): lax.all_to_all(along_y, 'sx', split_axis=3, concat_axis=2, tiled=True)  16.7 us
    all_to_all x1, starting transfers between devices, switch_the_masks(): step_out = all_to_all(z, ax_name, 0, 0)  9.14 us
    dot_general x1, matrix products, body(): jnp.einsum(pattern, backward[:, 0], forward[:, 1], preferred_element_type...  7.53 us
    all_to_all x1, other arithmetic, switch_the_masks(): step_out = all_to_all(z, ax_name, 0, 0)  7.32 us
    dot_general x1, matrix products, body(): jnp.einsum(pattern, backward[:, 1], forward[:, 1], preferred_element_type...  5.64 us
  transfers between devices with their start and end apart: 2, of which 1 were waited for; matrix products, arithmetic and copies ran while one was open for 2% of the time, Pallas kernels for 0%

profile of v1, /device:TPU:1, one launch (start us, length us, event | category | flops | bytes accessed | tf_op | source)
XLA Modules:
  0.0 277.6 jit_solution(15155843826917794315)
XLA Ops:
  0.6 0.7 fusion.96
  1.3 2.1 reshape.381
  3.4 0.8 fusion.148
  4.3 4.5 %copy.74 = bf16[2,1,4,3,12,512]{4,2,3,5,0,1:T(4,128)(2,1)S(1)} copy(bf16[2,1,4,3,12,512]{5,4,3,2,1,0:T(8,128)(2,1)} %get-tuple-element.11) | data formatting | bytes 589824
  8.7 2.8 %reshape.382 = bf16[2,2,4,3,12,512]{5,4,3,2,1,0:T(8,128)(2,1)} reshape(bf16[2,2,12,12,2,256]{5,4,3,2,1,0:T(2,128)(2,1)} %param.6) | data formatting | bytes 1179648 | tf_op jit(solution)/shard_map/reshape | solution.py:114
  11.5 2.1 fusion.149
  13.6 5.2 %copy.75 = bf16[2,1,4,3,12,512]{4,2,3,5,0,1:T(4,128)(2,1)} copy(bf16[2,1,4,3,12,512]{5,4,3,2,1,0:T(8,128)(2,1)} %get-tuple-element.13) | data formatting | bytes 589824
  18.8 3.8 %copy.72 = bf16[2,1,4,3,12,512]{4,2,3,5,0,1:T(4,128)(2,1)} copy(bf16[2,1,4,3,12,512]{5,4,3,2,1,0:T(8,128)(2,1)S(1)} %get-tuple-element.10) | data formatting | bytes 589824
  22.6 5.3 %copy.73 = bf16[2,1,4,3,12,512]{4,2,3,5,0,1:T(4,128)(2,1)} copy(bf16[2,1,4,3,12,512]{5,4,3,2,1,0:T(8,128)(2,1)} %get-tuple-element.12) | data formatting | bytes 589824
  27.9 5.6 %fusion.2 = f32[2,512,4,4,1]{3,2,4,1,0:T(4,128)S(1)} fusion(bf16[2,1,4,3,12,512]{4,2,3,5,0,1:T(4,128)(2,1)} %copy.75, bf16[2,1,4,3,12,512]{4,2,3,5,0,1:T(4,128)(2,1)S(1)} %copy.74), kind=kOutput, calls=%fused_computation.2 | convolution fusion | flops 1179648 | bytes 655360 | tf_op jit(solution)/shard_map/tscjn,tucjn->sutn/dot_general | solution.py:118
  33.6 5.0 %fusion = f32[2,512,4,4,1]{3,2,4,1,0:T(4,128)} fusion(bf16[2,1,4,3,12,512]{4,2,3,5,0,1:T(4,128)(2,1)S(1)} %copy-done.2, bf16[2,1,4,3,12,512]{4,2,3,5,0,1:T(4,128)(2,1)S(1)} %copy-done.3), kind=kOutput, calls=%fused_computation | convolution fusion | flops 1179648 | bytes 655360 | tf_op jit(solution)/shard_map/tscjn,tucjn->sutn/dot_general | solution.py:121
  38.6 3.7 %fusion.13 = f32[4,4,2,512]{0,1,3,2:T(4,128)} fusion(f32[2,512,4,4,1]{3,2,4,1,0:T(4,128)S(1)} %fusion.2, bf16[2,1,4,3,12,512]{4,2,3,5,0,1:T(4,128)(2,1)S(1)} %copy-done.1, bf16[2,1,4,3,12,512]{4,2,3,5,0,1:T(4,128)(2,1)S(1)} %copy-done.3), kind=kOutput, calls=%fused_computation.15 | convolution fusion | flops 1196032 | bytes 720896 | tf_op jit(solution)/shard_map/tscjn,tucjn->sutn/dot_general | solution.py:116
  42.2 2.1 copy.42
  44.4 7.5 %fusion.12 = f32[4,4,2,512]{0,1,3,2:T(4,128)} fusion(f32[2,512,4,4,1]{3,2,4,1,0:T(4,128)} %fusion, bf16[2,1,4,3,12,512]{4,2,3,5,0,1:T(4,128)(2,1)} %copy.73, bf16[2,1,4,3,12,512]{4,2,3,5,0,1:T(4,128)(2,1)S(1)} %copy.74), kind=kOutput, calls=%fused_computation.13 | convolution fusion | flops 1196032 | bytes 720896 | tf_op jit(solution)/shard_map/tscjn,tucjn->sutn/dot_general | solution.py:119
  51.9 1.9 copy.43
  55.4 1.3 and_select_fusion.1
  59.0 2.5 broadcast_bitcast_fusion
  61.5 5.5 %reshape.383 = f32[16,1,32768]{2,1,0:T(1,128)} reshape(f32[16,2,2,4,32,64]{5,4,3,2,1,0:T(8,128)} %broadcast_bitcast_fusion) | data formatting | bytes 4194304
  67.0 9.1 %all-to-all-start = ((f32[16,1,32768]{2,1,0:T(1,128)}), f32[16,1,32768]{2,1,0:T(1,128)S(1)}, u32[]{:S(2)}, u32[]{:S(2)}) async-start(f32[16,1,32768]{2,1,0:T(1,128)} %reshape.383), calls=%async_computation | async-start | bytes 4194304 | tf_op jit(solution)/shard_map/all_to_all | solution.py:15
  78.6 1.1 add_sine_fusion
  81.0 44.9 %all-to-all-done = f32[16,1,32768]{2,1,0:T(1,128)S(1)} async-done(((f32[16,1,32768]{2,1,0:T(1,128)}), f32[16,1,32768]{2,1,0:T(1,128)S(1)}, u32[]{:S(2)}, u32[]{:S(2)}) %all-to-all-start) | async-done | bytes 2097184 | tf_op jit(solution)/shard_map/all_to_all | solution.py:15
  125.9 1.3 copy-done
  127.8 7.3 %reduce = f32[16,32768]{1,0:T(8,128)S(1)} reduce(f32[16,1,32768]{2,1,0:T(1,128)} %copy-done, f32[]{:T(128)} %broadcast.524), dimensions={1}, to_apply=%all_to_all.16.reduce_sub_computation | reduce | bytes 4194308 | tf_op jit(solution)/shard_map/all_to_all | solution.py:15
  135.1 3.0 %reshape.384 = f32[16,2,2,4,32,64]{5,4,3,2,1,0:T(8,128)} reshape(f32[16,32768]{1,0:T(8,128)S(1)} %reduce) | data formatting | bytes 4194304
  138.1 2.7 copy.48
  140.8 2.5 constant_dynamic-slice_fusion.1
  143.3 2.6 copy.77
  146.9 1.2 copy.78
  149.4 1.0 reshape.385
  150.4 16.7 %all-to-all-start.1 = ((f32[32,1,1024]{2,1,0:T(1,128)}), f32[32,1,1024]{2,1,0:T(1,128)S(1)}, u32[]{:S(2)}, u32[]{:S(2)}) async-start(f32[32,1,1024]{2,1,0:T(1,128)} %reshape.385), calls=%async_computation.1 | async-start | bytes 262144 | tf_op jit(solution)/shard_map/all_to_all | solution.py:63
  167.4 104.0 %all-reduce = (f32[1,16,2,32]{3,2,1,0:T(2,128)S(1)}, f32[1,16,2,32]{3,2,1,0:T(2,128)S(1)}) all-reduce(f32[1,16,2,32]{3,2,1,0:T(2,128)S(1)} %bitcast.194, f32[1,16,2,32]{3,2,1,0:T(2,128)S(1)} %bitcast.193), channel_id=1, replica_groups=mesh['sx'=32,'sy'=16] {'sx','sy'}, use_global_device_ids=true, to_apply=%region_1.2 | all-reduce | flops 2048 | bytes 16384 | tf_op jit(solution)/shard_map/psum | solution.py:129
  272.0 1.0 reduce.1
  (67 shorter events, 15.8 us)
Async XLA Ops:
  27.9 5.6 %copy-start.2 = (bf16[2,1,4,3,12,512]{4,2,3,5,0,1:T(4,128)(2,1)S(1)}, bf16[2,1,4,3,12,512]{4,2,3,5,0,1:T(4,128)(2,1)}, u32[]{:S(2)}) copy-start(bf16[2,1,4,3,12,512]{4,2,3,5,0,1:T(4,128)(2,1)} %copy.75) | copy-start | bytes 884740
  27.9 5.6 %copy-start.3 = (bf16[2,1,4,3,12,512]{4,2,3,5,0,1:T(4,128)(2,1)S(1)}, bf16[2,1,4,3,12,512]{4,2,3,5,0,1:T(4,128)(2,1)}, u32[]{:S(2)}) copy-start(bf16[2,1,4,3,12,512]{4,2,3,5,0,1:T(4,128)(2,1)} %copy.72) | copy-start | bytes 884740
  33.6 5.0 %copy-start.1 = (bf16[2,1,4,3,12,512]{4,2,3,5,0,1:T(4,128)(2,1)S(1)}, bf16[2,1,4,3,12,512]{4,2,3,5,0,1:T(4,128)(2,1)}, u32[]{:S(2)}) copy-start(bf16[2,1,4,3,12,512]{4,2,3,5,0,1:T(4,128)(2,1)} %copy.73) | copy-start | bytes 884740
  44.3 9.5 %copy-start.4 = (s32[3]{0:T(128)S(1)}, s32[3]{0:T(128)}, u32[]{:S(2)}) copy-start(s32[3]{0:T(128)} %param.8) | copy-start | bytes 40
  44.4 10.2 %slice-start = ((s32[16,4,2]{0,2,1:T(2,128)}), s32[16,4,1]{0,2,1:T(1,128)S(1)}, s32[]{:S(2)}) async-start(s32[16,4,2]{0,2,1:T(2,128)} %param.7), calls=%async_computation.2 | async-start | bytes 4096 | tf_op jit(solution)/shard_map/slice | solution.py:21
  67.0 11.2 %copy-start.5 = (s32[32,3]{0,1:T(4,128)S(1)}, s32[32,3]{0,1:T(4,128)}, u32[]{:S(2)}) copy-start(s32[32,3]{0,1:T(4,128)} %param.9) | copy-start | bytes 1156
  67.0 58.9 %all-to-all-start = ((f32[16,1,32768]{2,1,0:T(1,128)}), f32[16,1,32768]{2,1,0:T(1,128)S(1)}, u32[]{:S(2)}, u32[]{:S(2)}) async-start(f32[16,1,32768]{2,1,0:T(1,128)} %reshape.383), calls=%async_computation | async-start | bytes 4194304 | tf_op jit(solution)/shard_map/all_to_all | solution.py:15
  125.9 1.3 copy-start
  150.4 121.7 %all-to-all-start.1 = ((f32[32,1,1024]{2,1,0:T(1,128)}), f32[32,1,1024]{2,1,0:T(1,128)S(1)}, u32[]{:S(2)}, u32[]{:S(2)}) async-start(f32[32,1,1024]{2,1,0:T(1,128)} %reshape.385), calls=%async_computation.1 | async-start | bytes 262144 | tf_op jit(solution)/shard_map/all_to_all | solution.py:63
